TPU v7x, 32 devices: a whole 2x2x4 slice. The times are simulated.
32 devices in a mesh: section: 2 (over core), seq: 4 (over y, x), tensor: 4 (over z).
Axes of the slice: x: 2, y: 2, z: 4, core: 2. Of those that a mesh axis runs over, the one named last changes fastest.
Arguments:
- tokens: bfloat16 [4096, 1024], P('seq', 'tensor'), may hold values from -6 to 6
- segments: int32 [8, 512], P('seq'), may hold values from 0 to 3, never falling along the last dimension, each value on 1 to 256 neighbouring positions
- cotangent: bfloat16 [4096, 1024], P('seq', 'tensor'), may hold values from -6 to 6
- norm1_gain: bfloat16 [2, 1024], P('section', ('tensor', 'seq')), may hold values from 0.5 to 1.5
- norm1_bias: bfloat16 [2, 1024], P('section', ('tensor', 'seq')), may hold values from -3 to 3
- qkv_weight: bfloat16 [2, 1024, 16, 192], P('section', 'seq', 'tensor'), may hold values from -0.1875 to 0.1875
- qv_bias: bfloat16 [2, 16, 128], P('section', 'tensor', 'seq'), may hold values from -4 to 4
- out_weight: bfloat16 [2, 16, 64, 1024], P('section', 'tensor', None, 'seq'), may hold values from -0.75 to 0.75
- out_bias: bfloat16 [2, 1024], P('section', ('tensor', 'seq')), may hold values from -3 to 3
- norm2_gain: bfloat16 [2, 1024], P('section', ('tensor', 'seq')), may hold values from 0.5 to 1.5
- norm2_bias: bfloat16 [2, 1024], P('section', ('tensor', 'seq')), may hold values from -3 to 3
- up_weight: bfloat16 [2, 1024, 4096], P('section', 'seq', 'tensor'), may hold values from -0.1875 to 0.1875
- up_bias: bfloat16 [2, 4096], P('section', ('tensor', 'seq')), may hold values from -4 to 4
- down_weight: bfloat16 [2, 4096, 1024], P('section', 'tensor', 'seq'), may hold values from -0.09375 to 0.09375
- down_bias: bfloat16 [2, 1024], P('section', ('tensor', 'seq')), may hold values from -3 to 3
Outputs:
- section_out: bfloat16 [2, 4096, 1024], P('section', 'seq', 'tensor')
- input_grad: bfloat16 [2, 4096, 1024], P('section', 'seq', 'tensor')
- grad_norm1_gain: float32 [2, 1024], P('section', ('tensor', 'seq'))
- grad_norm1_bias: float32 [2, 1024], P('section', ('tensor', 'seq'))
- grad_qkv_weight: float32 [2, 1024, 16, 192], P('section', 'seq', 'tensor')
- grad_qv_bias: float32 [2, 16, 128], P('section', 'tensor', 'seq')
- grad_out_weight: float32 [2, 16, 64, 1024], P('section', 'tensor', None, 'seq')
- grad_out_bias: float32 [2, 1024], P('section', ('tensor', 'seq'))
- grad_norm2_gain: float32 [2, 1024], P('section', ('tensor', 'seq'))
- grad_norm2_bias: float32 [2, 1024], P('section', ('tensor', 'seq'))
- grad_up_weight: float32 [2, 1024, 4096], P('section', 'seq', 'tensor')
- grad_up_bias: float32 [2, 4096], P('section', ('tensor', 'seq'))
- grad_down_weight: float32 [2, 4096, 1024], P('section', 'tensor', 'seq')
- grad_down_bias: float32 [2, 1024], P('section', ('tensor', 'seq'))
Inputs may be any that keep to these rules, and one draw needn't show every extreme that they name: `segments`: along each sequence the document numbers never fall; every document holds 1 to 256 positions.
All inputs are finite; a program needn't handle non-finite values.
Results may differ from a plain program's by a relative error of at most 0.02.
Values may be sent and summed in bfloat16 or wider, within the bound.
A program may use at most 192 MiB of HBM per device.

v0:
```python
import functools
import math
import jax
import jax.numpy as jnp
from jax import lax
from jax.sharding import PartitionSpec as P

epsilon = 1e-05
floor_value = -1e30
f32 = jnp.float32
bf16 = jnp.bfloat16


def gather_columns(piece):
    return lax.all_gather(piece, "tensor", axis=1, tiled=True)


def gather_rows(piece):
    return lax.all_gather(piece, "tensor", axis=0, tiled=True)


def scatter_rows(partial_rows):
    return lax.psum_scatter(
        partial_rows.astype(bf16), "tensor", scatter_dimension=0, tiled=True
    ).astype(f32)


def norm_parts(rows):
    average = jnp.mean(rows, axis=1, keepdims=True)
    variance = jnp.mean(rows * rows, axis=1, keepdims=True) - average * average
    scale = lax.rsqrt(variance + epsilon)
    return ((rows - average) * scale, scale)


def norm_backward(grad, centred, scale, gain):
    scaled = grad * gain
    total = jnp.mean(scaled, axis=1, keepdims=True)
    along = jnp.mean(scaled * centred, axis=1, keepdims=True)
    return scale * (scaled - total - centred * along)


def allowed_mask(segment):
    length = segment.shape[1]
    place = lax.broadcasted_iota(jnp.int32, (length, length), 0)
    other = lax.broadcasted_iota(jnp.int32, (length, length), 1)
    same = segment[:, :, None] == segment[:, None, :]
    return (same & (other <= place)[None])[:, None]


def gelu_value(upper):
    return jax.nn.gelu(upper, approximate=True)


def dot(left, right, dims):
    return lax.dot_general(left, right, (dims, ((), ())), preferred_element_type=f32)


def forward(whole, rows, mask, weights):
    gain1, bias1, w_qkv, b_qv, w_out, b_out, gain2, bias2, w_up, b_up, w_down, b_down = weights
    count = whole.shape[0]
    heads, wide = w_qkv.shape[1:]
    size = wide // 3
    shape4 = (mask.shape[0], mask.shape[2], heads, size)
    factor = 1.0 / math.sqrt(size)
    normed = (norm_parts(whole.astype(f32))[0] * gain1 + bias1).astype(bf16)
    rows = rows.astype(f32)
    centred1, scale1 = norm_parts(rows)
    mixed = jnp.einsum("rd,dhe->rhe", normed, w_qkv, preferred_element_type=f32)
    query = (mixed[..., :size] + b_qv[:, :size]).astype(bf16).reshape(shape4)
    keys = mixed[..., size : 2 * size].astype(bf16).reshape(shape4)
    values = (mixed[..., 2 * size :] + b_qv[:, size:]).astype(bf16).reshape(shape4)
    scores = jnp.einsum("sqhe,skhe->shqk", query, keys, preferred_element_type=f32) * factor
    masked = jnp.where(mask, scores, floor_value)
    raised = jnp.exp(masked - jnp.max(masked, axis=-1, keepdims=True))
    chance = raised / jnp.sum(raised, axis=-1, keepdims=True)
    low = chance.astype(bf16)
    context = jnp.einsum("shqk,skhe->sqhe", low, values, preferred_element_type=f32)
    context = context.reshape(count, heads * size).astype(bf16)
    attn = scatter_rows(dot(context, w_out, ((1,), (0,)))) + b_out
    hidden = rows + attn
    centred2, scale2 = norm_parts(hidden)
    normed2 = gather_rows((centred2 * gain2 + bias2).astype(bf16))
    upper = dot(normed2, w_up, ((1,), (0,))) + b_up
    active = gelu_value(upper).astype(bf16)
    branch = scatter_rows(dot(active, w_down, ((1,), (0,)))) + b_down
    output = (hidden + branch).astype(bf16)
    kept = (
        centred1,
        scale1,
        normed,
        query,
        keys,
        values,
        chance,
        low,
        context,
        centred2,
        scale2,
        normed2,
        upper,
        active,
    )
    return (output, kept)


def backward(grad_whole, grad_rows, weights, kept):
    gain1, bias1, w_qkv, b_qv, w_out, b_out, gain2, bias2, w_up, b_up, w_down, b_down = weights
    (
        centred1,
        scale1,
        normed,
        query,
        keys,
        values,
        chance,
        low,
        context,
        centred2,
        scale2,
        normed2,
        upper,
        active,
    ) = kept
    count = grad_whole.shape[0]
    heads, wide = w_qkv.shape[1:]
    size = wide // 3
    factor = 1.0 / math.sqrt(size)
    grad_out = grad_rows.astype(f32)
    grad_active = dot(grad_whole, w_down, ((1,), (1,)))
    grad_upper = jax.vjp(gelu_value, upper)[1](grad_active)[0].astype(bf16)
    grad_normed2 = scatter_rows(dot(grad_upper, w_up, ((1,), (1,))))
    grad_down = dot(active, grad_whole, ((0,), (0,)))
    grad_up = dot(normed2, grad_upper, ((0,), (0,)))
    grad_hidden = grad_out + norm_backward(grad_normed2, centred2, scale2, gain2)
    grad_attn = grad_hidden.astype(bf16)
    attn_whole = gather_rows(grad_attn)
    grad_context = dot(attn_whole, w_out, ((1,), (1,))).astype(bf16).reshape(query.shape)
    grad_out_w = dot(context, attn_whole, ((0,), (0,)))
    grad_chance = jnp.einsum("sqhe,skhe->shqk", grad_context, values, preferred_element_type=f32)
    delta = jnp.sum(grad_chance * chance, axis=-1, keepdims=True)
    grad_scores = (chance * (grad_chance - delta)).astype(bf16)
    grad_query = (
        jnp.einsum("shqk,skhe->sqhe", grad_scores, keys, preferred_element_type=f32) * factor
    ).astype(bf16)
    grad_keys = (
        jnp.einsum("shqk,sqhe->skhe", grad_scores, query, preferred_element_type=f32) * factor
    ).astype(bf16)
    grad_values = jnp.einsum(
        "shqk,sqhe->skhe", low, grad_context, preferred_element_type=f32
    ).astype(bf16)
    grad_mixed = jnp.concatenate([grad_query, grad_keys, grad_values], axis=-1).reshape(
        count, heads, wide
    )
    grad_normed1 = scatter_rows(
        jnp.einsum("rhe,dhe->rd", grad_mixed, w_qkv, preferred_element_type=f32)
    )
    grad_qkv = jnp.einsum("rd,rhe->dhe", normed, grad_mixed, preferred_element_type=f32)
    grad_qv = jnp.concatenate(
        [
            jnp.sum(grad_query.astype(f32), axis=(0, 1)),
            jnp.sum(grad_values.astype(f32), axis=(0, 1)),
        ],
        axis=-1,
    )
    grad_input = grad_hidden + norm_backward(grad_normed1, centred1, scale1, gain1)
    vectors = (
        jnp.sum(grad_normed1 * centred1, axis=0),
        jnp.sum(grad_normed1, axis=0),
        jnp.sum(grad_attn.astype(f32), axis=0),
        jnp.sum(grad_normed2 * centred2, axis=0),
        jnp.sum(grad_normed2, axis=0),
        jnp.sum(grad_out, axis=0),
    )
    local = (jnp.sum(grad_upper.astype(f32), axis=0), grad_qv)
    return (grad_input.astype(bf16), (grad_qkv, grad_out_w, grad_up, grad_down), vectors, local)


def swap(item):
    return lax.ppermute(item, "section", [(0, 1), (1, 0)])


def body(
    tokens,
    segments,
    cotangent,
    norm1_gain,
    norm1_bias,
    qkv_weight,
    qv_bias,
    out_weight,
    out_bias,
    norm2_gain,
    norm2_bias,
    up_weight,
    up_bias,
    down_weight,
    down_bias,
):
    section = lax.axis_index("section")
    place = lax.axis_index("tensor")
    tensors = lax.axis_size("tensor")
    quads = lax.axis_size("seq")
    first = section == 0
    rows_all, width = tokens.shape
    count = rows_all // 2
    block = count // tensors
    full = width * tensors
    heads, wide = qkv_weight.shape[2:]
    size = wide // 3
    part = norm1_gain.shape[1]
    part_up = up_bias.shape[1]
    part_qv = qv_bias.shape[2]

    def mine(item):
        return lax.dynamic_slice_in_dim(item, section * (item.shape[0] // 2), item.shape[0] // 2, 0)

    def block_of(whole):
        return lax.dynamic_slice_in_dim(whole, place * block, block, 0)

    def columns_of(whole):
        return lax.dynamic_slice_in_dim(whole, place * width, width, 1)

    whole0 = gather_columns(mine(tokens))
    packed = jnp.concatenate(
        [
            norm1_gain[0],
            norm1_bias[0],
            out_bias[0],
            norm2_gain[0],
            norm2_bias[0],
            down_bias[0],
            up_bias[0],
            qv_bias[0].reshape(-1),
        ]
    )
    small = lax.all_gather(packed, ("section", "tensor", "seq"), axis=0, tiled=False)
    small = small.reshape(2, tensors, quads, packed.shape[0]).astype(f32)

    def pair(weight, axis):
        gathered = lax.all_gather(weight, "seq", axis=axis, tiled=True)
        return lax.all_gather(gathered, "section", axis=0, tiled=False)

    w_qkv = pair(qkv_weight[0], 0)
    w_out = pair(out_weight[0].reshape(heads * size, -1), 1)
    w_up = pair(up_weight[0], 0)
    w_down = pair(down_weight[0], 1)
    whole_cot = gather_columns(mine(cotangent))

    def weights_of(layer):
        own = small[layer]
        vectors = [own[:, :, i * part : (i + 1) * part].reshape(full) for i in range(6)]
        local = lax.dynamic_slice_in_dim(own, place, 1, 0)[0]
        b_up = local[:, 6 * part : 6 * part + part_up].reshape(-1)
        b_qv = local[:, 6 * part + part_up :].reshape(quads, heads, part_qv)
        b_qv = jnp.transpose(b_qv, (1, 0, 2)).reshape(heads, 2 * size)
        return (
            vectors[0],
            vectors[1],
            w_qkv[layer],
            b_qv,
            w_out[layer],
            vectors[2],
            vectors[3],
            vectors[4],
            w_up[layer],
            b_up,
            w_down[layer],
            vectors[5],
        )

    params = (weights_of(0), weights_of(1))
    mask = allowed_mask(mine(segments))
    out0, kept0 = forward(whole0, block_of(whole0), mask, params[0])
    whole1 = gather_rows(out0)
    out1, kept1 = forward(whole1, out0, mask, params[1])
    grad1, big1, vec1, loc1 = backward(whole_cot, block_of(whole_cot), params[1], kept1)

    def reduce_big(big):
        axes = (0, 1, 0, 1)
        return tuple(
            (
                lax.psum_scatter(item.astype(bf16), "seq", scatter_dimension=axis, tiled=True)
                for item, axis in zip(big, axes)
            )
        )

    red1 = reduce_big(big1)
    whole_grad = gather_rows(grad1)
    grad0, big0, vec0, loc0 = backward(whole_grad, grad1, params[0], kept0)
    red0 = reduce_big(big0)

    def to_columns(rows):
        return lax.all_to_all(rows, "tensor", split_axis=1, concat_axis=0, tiled=True)

    def settle(of0, of1):
        own = jnp.where(first, of0, of1)
        other = swap(jnp.where(first, of1, of0))
        return jnp.where(first, jnp.concatenate([own, other]), jnp.concatenate([other, own]))

    outputs = settle(columns_of(whole1), to_columns(out1))
    input_grads = settle(to_columns(grad0), columns_of(whole_grad))
    totals = tuple(
        (
            jnp.where(first, a, b).astype(f32) + swap(jnp.where(first, b, a)).astype(f32)
            for a, b in zip(red0, red1)
        )
    )

    def pack(vectors, local):
        rows = [item.reshape(tensors, quads, part) for item in vectors]
        up = local[0].reshape(1, quads, part_up)
        qv = jnp.transpose(local[1].reshape(heads, quads, part_qv), (1, 0, 2))
        here = jnp.concatenate([up, qv.reshape(1, quads, heads * part_qv)], axis=-1)
        ours = lax.broadcasted_iota(jnp.int32, (tensors, 1, 1), 0) == place
        rows.append(jnp.where(ours, here, 0.0))
        return jnp.concatenate(rows, axis=-1)

    vectors = jnp.stack([pack(vec0, loc0), pack(vec1, loc1)])
    vectors = vectors.reshape(2 * tensors * quads, -1)
    vectors = lax.psum_scatter(
        vectors, ("section", "tensor", "seq"), scatter_dimension=0, tiled=True
    )[0]
    small_grads = [vectors[i * part : (i + 1) * part] for i in range(6)]
    g_up = vectors[6 * part : 6 * part + part_up]
    g_qv = vectors[6 * part + part_up :].reshape(heads, part_qv)
    result = (
        outputs,
        input_grads,
        small_grads[0],
        small_grads[1],
        totals[0],
        g_qv,
        totals[1].reshape(heads, size, -1),
        small_grads[2],
        small_grads[3],
        small_grads[4],
        totals[2],
        g_up,
        totals[3],
        small_grads[5],
    )
    return tuple((item[None] for item in result))


def solution(mesh):
    return jax.shard_map(
        body,
        mesh=mesh,
        in_specs=(
            P("seq", "tensor"),
            P("seq", None),
            P("seq", "tensor"),
            P("section", ("tensor", "seq")),
            P("section", ("tensor", "seq")),
            P("section", "seq", "tensor", None),
            P("section", "tensor", "seq"),
            P("section", "tensor", None, "seq"),
            P("section", ("tensor", "seq")),
            P("section", ("tensor", "seq")),
            P("section", ("tensor", "seq")),
            P("section", "seq", "tensor"),
            P("section", ("tensor", "seq")),
            P("section", "tensor", "seq"),
            P("section", ("tensor", "seq")),
        ),
        out_specs=(
            P("section", "seq", "tensor"),
            P("section", "seq", "tensor"),
            P("section", ("tensor", "seq")),
            P("section", ("tensor", "seq")),
            P("section", "seq", "tensor", None),
            P("section", "tensor", "seq"),
            P("section", "tensor", None, "seq"),
            P("section", ("tensor", "seq")),
            P("section", ("tensor", "seq")),
            P("section", ("tensor", "seq")),
            P("section", "seq", "tensor"),
            P("section", ("tensor", "seq")),
            P("section", "tensor", "seq"),
            P("section", ("tensor", "seq")),
        ),
        check_vma=False,
    )
```

profile of v0, /device:TPU:8, one launch (start us, length us, event | category | flops | bytes accessed | tf_op | source)
XLA Modules:
  0.0 1104.5 jit_solution(2725057039113949337)
XLA Ops:
  9.0 32.7 %all-gather.41.cloned.1.call-done = bf16[1,1024,4,192]{1,3,2,0:T(8,128)(2,1)} async-done(((bf16[1,256,4,192]{1,3,2,0:T(8,128)(2,1)}), bf16[1,1024,4,192]{1,3,2,0:T(8,128)(2,1)}) %all-gather.41.cloned.1.call-update) | async-done | bytes 1572880 | tf_op jit(solution)/shard_map/all_gather | solution.py:240
  41.8 13.8 %all_gather.72 = bf16[256,1024]{1,0:T(8,128)(2,1)} all-gather(bf16[256,256]{1,0:T(8,128)(2,1)S(1)} %bitcast.220), channel_id=1, replica_groups=mesh['section'=2,'seq'=4,'tensor'=4] {'seq'}, dimensions={1}, use_global_device_ids=true | all-gather | bytes 655360 | tf_op jit(solution)/shard_map/all_gather | solution.py:240
  56.5 62.1 %all-gather.8 = bf16[32,1,768]{2,1,0:T(2,128)(2,1)S(1)} all-gather(bf16[1,1,768]{2,1,0:T(2,128)(2,1)S(1)} %reshape.655), channel_id=2, replica_groups=mesh['section'=2,'seq'=4,'tensor'=4] {'section','tensor','seq'}, dimensions={0}, use_global_device_ids=true | all-gather | bytes 50688 | tf_op jit(solution)/shard_map/all_gather | solution.py:236
  138.8 25.6 %reduce-scatter.17.cloned.1.call-done = bf16[128,1024]{1,0:T(8,128)(2,1)} async-done(((bf16[512,1024]{1,0:T(8,128)(2,1)}), bf16[128,1024]{1,0:T(8,128)(2,1)}) %reduce-scatter.17.cloned.1.call-update) | async-done | bytes 262160 | tf_op jit(solution)/shard_map/reduce_scatter | solution.py:23
  167.5 34.4 %all-gather.51.cloned.1.call-done = bf16[1,1024,1024]{2,1,0:T(8,128)(2,1)} async-done(((bf16[1,1024,256]{2,1,0:T(8,128)(2,1)}), bf16[1,1024,1024]{2,1,0:T(8,128)(2,1)}) %all-gather.51.cloned.1.call-update) | async-done | bytes 2097168 | tf_op jit(solution)/shard_map/all_gather | solution.py:240
  202.0 15.4 %all-gather.49.cloned.1.call-done = bf16[2,1024,1024]{2,1,0:T(8,128)(2,1)} async-done(((bf16[1,1024,1024]{2,1,0:T(8,128)(2,1)}), bf16[2,1024,1024]{2,1,0:T(8,128)(2,1)}) %all-gather.49.cloned.1.call-update) | async-done | bytes 4194320 | tf_op jit(solution)/shard_map/all_gather | solution.py:241
  217.4 31.0 %all-gather.27.cloned.1.call-done = bf16[512,1024]{1,0:T(8,128)(2,1)} async-done(((bf16[128,1024]{1,0:T(8,128)(2,1)}), bf16[512,1024]{1,0:T(8,128)(2,1)}) %all-gather.27.cloned.1.call-update) | async-done | bytes 1048592 | tf_op jit(solution)/shard_map/all_gather | solution.py:19
  253.0 10.3 all-gather.53.cloned.1.call-done
  268.1 26.2 %reduce-scatter.19.cloned.1.call-done = bf16[128,1024]{1,0:T(8,128)(2,1)} async-done(((bf16[512,1024]{1,0:T(8,128)(2,1)}), bf16[128,1024]{1,0:T(8,128)(2,1)}) %reduce-scatter.19.cloned.1.call-update) | async-done | bytes 262160 | tf_op jit(solution)/shard_map/reduce_scatter | solution.py:23
  297.3 27.6 %all-gather.29.cloned.1.call-done = bf16[512,1024]{1,0:T(8,128)(2,1)} async-done(((bf16[128,1024]{1,0:T(8,128)(2,1)}), bf16[512,1024]{1,0:T(8,128)(2,1)}) %all-gather.29.cloned.1.call-update) | async-done | bytes 1048592 | tf_op jit(solution)/shard_map/all_gather | solution.py:19
  339.6 24.5 %reduce-scatter.21.cloned.1.call-done = bf16[128,1024]{1,0:T(8,128)(2,1)} async-done(((bf16[512,1024]{1,0:T(8,128)(2,1)}), bf16[128,1024]{1,0:T(8,128)(2,1)}) %reduce-scatter.21.cloned.1.call-update) | async-done | bytes 262160 | tf_op jit(solution)/shard_map/reduce_scatter | solution.py:23
  368.0 27.8 %all-gather.31.cloned.1.call-done = bf16[512,1024]{1,0:T(8,128)(2,1)} async-done(((bf16[128,1024]{1,0:T(8,128)(2,1)}), bf16[512,1024]{1,0:T(8,128)(2,1)}) %all-gather.31.cloned.1.call-update) | async-done | bytes 1048592 | tf_op jit(solution)/shard_map/all_gather | solution.py:19
  400.3 27.9 %all-gather.33.cloned.1.call-done = bf16[512,1024]{1,0:T(8,128)(2,1)} async-done(((bf16[512,256]{1,0:T(8,128)(2,1)}), bf16[512,1024]{1,0:T(8,128)(2,1)}) %all-gather.33.cloned.1.call-update) | async-done | bytes 1048592 | tf_op jit(solution)/shard_map/all_gather | solution.py:15
  428.2 5.2 convert_reduce_fusion.2
  441.6 17.7 %reduce-scatter.25.cloned.1.call-done = bf16[128,1024]{1,0:T(8,128)(2,1)} async-done(((bf16[512,1024]{1,0:T(8,128)(2,1)}), bf16[128,1024]{1,0:T(8,128)(2,1)}) %reduce-scatter.25.cloned.1.call-update) | async-done | bytes 262160 | tf_op jit(solution)/shard_map/reduce_scatter | solution.py:23
  460.6 27.2 %reduce-scatter.23.cloned.1.call-done = bf16[128,1024]{1,0:T(8,128)(2,1)} async-done(((bf16[512,1024]{1,0:T(8,128)(2,1)}), bf16[128,1024]{1,0:T(8,128)(2,1)}) %reduce-scatter.23.cloned.1.call-update) | async-done | bytes 262160 | tf_op jit(solution)/shard_map/reduce_scatter | solution.py:23
  490.3 28.4 %all-gather.35.cloned.1.call-done = bf16[512,1024]{1,0:T(8,128)(2,1)} async-done(((bf16[128,1024]{1,0:T(8,128)(2,1)}), bf16[512,1024]{1,0:T(8,128)(2,1)}) %all-gather.35.cloned.1.call-update) | async-done | bytes 1048592 | tf_op jit(solution)/shard_map/all_gather | solution.py:19
  530.7 24.7 %reduce-scatter.27.cloned.1.call-done = bf16[128,1024]{1,0:T(8,128)(2,1)} async-done(((bf16[512,1024]{1,0:T(8,128)(2,1)}), bf16[128,1024]{1,0:T(8,128)(2,1)}) %reduce-scatter.27.cloned.1.call-update) | async-done | bytes 262160 | tf_op jit(solution)/shard_map/reduce_scatter | solution.py:23
  558.6 28.6 %all-gather.37.cloned.1.call-done = bf16[512,1024]{1,0:T(8,128)(2,1)} async-done(((bf16[128,1024]{1,0:T(8,128)(2,1)}), bf16[512,1024]{1,0:T(8,128)(2,1)}) %all-gather.37.cloned.1.call-update) | async-done | bytes 1048592 | tf_op jit(solution)/shard_map/all_gather | solution.py:19
  595.7 24.7 %reduce-scatter.29.cloned.1.call-done = bf16[128,1024]{1,0:T(8,128)(2,1)} async-done(((bf16[512,1024]{1,0:T(8,128)(2,1)}), bf16[128,1024]{1,0:T(8,128)(2,1)}) %reduce-scatter.29.cloned.1.call-update) | async-done | bytes 262160 | tf_op jit(solution)/shard_map/reduce_scatter | solution.py:23
  643.0 10.0 all-gather.39.cloned.1.call-done
  677.9 6.3 all-to-all-done
  693.5 35.1 %reduce-scatter.45.cloned.1.call-done = bf16[1024,256]{1,0:T(8,128)(2,1)} async-done(((bf16[1024,1024]{1,0:T(8,128)(2,1)}), bf16[1024,256]{1,0:T(8,128)(2,1)}) %reduce-scatter.45.cloned.1.call-update) | async-done | bytes 524304 | tf_op jit(solution)/shard_map/reduce_scatter | solution.py:282
  730.8 36.0 %reduce-scatter.43.cloned.1.call-done = bf16[256,1024]{1,0:T(8,128)(2,1)} async-done(((bf16[1024,1024]{1,0:T(8,128)(2,1)}), bf16[256,1024]{1,0:T(8,128)(2,1)}) %reduce-scatter.43.cloned.1.call-update) | async-done | bytes 524304 | tf_op jit(solution)/shard_map/reduce_scatter | solution.py:282
  766.8 38.0 %reduce-scatter.41.cloned.1.call-done = bf16[256,1024]{1,0:T(8,128)(2,1)} async-done(((bf16[1024,1024]{1,0:T(8,128)(2,1)}), bf16[256,1024]{1,0:T(8,128)(2,1)}) %reduce-scatter.41.cloned.1.call-update) | async-done | bytes 524304 | tf_op jit(solution)/shard_map/reduce_scatter | solution.py:282
  808.3 24.6 %reduce-scatter.31.cloned.1.call-done = bf16[128,1024]{1,0:T(8,128)(2,1)} async-done(((bf16[512,1024]{1,0:T(8,128)(2,1)}), bf16[128,1024]{1,0:T(8,128)(2,1)}) %reduce-scatter.31.cloned.1.call-update) | async-done | bytes 262160 | tf_op jit(solution)/shard_map/reduce_scatter | solution.py:23
  836.0 6.0 all-to-all-start.1
  844.3 17.6 %reduce-scatter.39.cloned.1.call-done = bf16[256,256]{1,0:T(8,128)(2,1)} async-done(((bf16[256,1024]{1,0:T(8,128)(2,1)}), bf16[256,256]{1,0:T(8,128)(2,1)}) %reduce-scatter.39.cloned.1.call-update) | async-done | bytes 131088 | tf_op jit(solution)/shard_map/reduce_scatter | solution.py:282
  861.9 28.5 %reduce-scatter.37.cloned.1.call-done = bf16[256,256]{1,0:T(8,128)(2,1)} async-done(((bf16[256,1024]{1,0:T(8,128)(2,1)}), bf16[256,256]{1,0:T(8,128)(2,1)}) %reduce-scatter.37.cloned.1.call-update) | async-done | bytes 131088 | tf_op jit(solution)/shard_map/reduce_scatter | solution.py:282
  894.1 30.3 %reduce-scatter.35.cloned.1.call-done = bf16[256,4,192]{0,2,1:T(8,128)(2,1)} async-done(((bf16[1024,4,192]{0,2,1:T(8,128)(2,1)}), bf16[256,4,192]{0,2,1:T(8,128)(2,1)}) %reduce-scatter.35.cloned.1.call-update) | async-done | bytes 393232 | tf_op jit(solution)/shard_map/reduce_scatter | solution.py:282
  924.5 34.2 %reduce-scatter.33.cloned.1.call-done = bf16[256,4,192]{0,2,1:T(8,128)(2,1)} async-done(((bf16[1024,4,192]{0,2,1:T(8,128)(2,1)}), bf16[256,4,192]{0,2,1:T(8,128)(2,1)}) %reduce-scatter.33.cloned.1.call-update) | async-done | bytes 393232 | tf_op jit(solution)/shard_map/reduce_scatter | solution.py:282
  960.6 128.7 %all-reduce.3.cloned.1.call-done = f32[32,768]{1,0:T(8,128)} async-done(((f32[32,768]{1,0:T(8,128)}), f32[32,768]{1,0:T(8,128)}) %all-reduce.3.cloned.1.call-update) | async-done | bytes 98320
  (365 shorter events, 177.9 us)
Async XLA Ops:
  8.0 111.8 %all-gather.25.cloned.1.call-start = ((), (), s32[]{:S(2)}) async-start(), calls=%async_computation.18 | async-start | bytes 1310720 | tf_op jit(solution)/shard_map/all_gather | solution.py:15
  9.0 112.6 %all-gather.43.cloned.1.call-start = ((), (), s32[]{:S(2)}) async-start(), calls=%async_computation.43 | async-start | bytes 4718592 | tf_op jit(solution)/shard_map/all_gather | solution.py:241
  41.8 92.7 %all-gather.45.cloned.1.call-start = ((), (), s32[]{:S(2)}) async-start(), calls=%async_computation.44 | async-start | bytes 1572864 | tf_op jit(solution)/shard_map/all_gather | solution.py:241
  55.6 82.2 %all-gather.47.cloned.1.call-start = ((), (), s32[]{:S(2)}) async-start(), calls=%async_computation.45 | async-start | bytes 2621440 | tf_op jit(solution)/shard_map/all_gather | solution.py:240
  56.2 108.2 %reduce-scatter.17.cloned.1.call-start = ((), (), s32[]{:S(2)}) async-start(), calls=%async_computation.19 | async-start | bytes 1310720 | tf_op jit(solution)/shard_map/reduce_scatter | solution.py:23
  137.0 64.9 %all-gather.51.cloned.1.call-start = ((), (), s32[]{:S(2)}) async-start(), calls=%async_computation.47 | async-start | bytes 2621440 | tf_op jit(solution)/shard_map/all_gather | solution.py:240
  137.8 79.6 %all-gather.49.cloned.1.call-start = ((), (), s32[]{:S(2)}) async-start(), calls=%async_computation.46 | async-start | bytes 6291456 | tf_op jit(solution)/shard_map/all_gather | solution.py:241
  138.5 109.9 %all-gather.27.cloned.1.call-start = ((), (), s32[]{:S(2)}) async-start(), calls=%async_computation.20 | async-start | bytes 1310720 | tf_op jit(solution)/shard_map/all_gather | solution.py:19
  167.4 95.8 %all-gather.53.cloned.1.call-start = ((), (), s32[]{:S(2)}) async-start(), calls=%async_computation.48 | async-start | bytes 6291456 | tf_op jit(solution)/shard_map/all_gather | solution.py:241
  201.9 92.4 %reduce-scatter.19.cloned.1.call-start = ((), (), s32[]{:S(2)}) async-start(), calls=%async_computation.21 | async-start | bytes 1310720 | tf_op jit(solution)/shard_map/reduce_scatter | solution.py:23
  268.0 56.8 %all-gather.29.cloned.1.call-start = ((), (), s32[]{:S(2)}) async-start(), calls=%async_computation.22 | async-start | bytes 1310720 | tf_op jit(solution)/shard_map/all_gather | solution.py:19
  296.1 68.0 %reduce-scatter.21.cloned.1.call-start = ((), (), s32[]{:S(2)}) async-start(), calls=%async_computation.23 | async-start | bytes 1310720 | tf_op jit(solution)/shard_map/reduce_scatter | solution.py:23
  367.1 61.1 %all-gather.33.cloned.1.call-start = ((), (), s32[]{:S(2)}) async-start(), calls=%async_computation.26 | async-start | bytes 1310720 | tf_op jit(solution)/shard_map/all_gather | solution.py:15
  367.9 91.3 %reduce-scatter.25.cloned.1.call-start = ((), (), s32[]{:S(2)}) async-start(), calls=%async_computation.27 | async-start | bytes 1310720 | tf_op jit(solution)/shard_map/reduce_scatter | solution.py:23
  441.5 77.3 %all-gather.35.cloned.1.call-start = ((), (), s32[]{:S(2)}) async-start(), calls=%async_computation.28 | async-start | bytes 1310720 | tf_op jit(solution)/shard_map/all_gather | solution.py:19
  490.1 65.3 %reduce-scatter.27.cloned.1.call-start = ((), (), s32[]{:S(2)}) async-start(), calls=%async_computation.29 | async-start | bytes 1310720 | tf_op jit(solution)/shard_map/reduce_scatter | solution.py:23
  558.6 61.9 %reduce-scatter.29.cloned.1.call-start = ((), (), s32[]{:S(2)}) async-start(), calls=%async_computation.31 | async-start | bytes 1310720 | tf_op jit(solution)/shard_map/reduce_scatter | solution.py:23
  595.7 57.3 %all-gather.39.cloned.1.call-start = ((), (), s32[]{:S(2)}) async-start(), calls=%async_computation.32 | async-start | bytes 1310720 | tf_op jit(solution)/shard_map/all_gather | solution.py:19
  624.4 69.2 %reduce-scatter.47.cloned.1.call-start = ((), (), s32[]{:S(2)}) async-start(), calls=%async_computation.41 | async-start | bytes 2621440 | tf_op jit(solution)/shard_map/reduce_scatter | solution.py:282
  629.2 99.4 %reduce-scatter.45.cloned.1.call-start = ((), (), s32[]{:S(2)}) async-start(), calls=%async_computation.40 | async-start | bytes 2621440 | tf_op jit(solution)/shard_map/reduce_scatter | solution.py:282
  634.4 132.4 %reduce-scatter.43.cloned.1.call-start = ((), (), s32[]{:S(2)}) async-start(), calls=%async_computation.39 | async-start | bytes 2621440 | tf_op jit(solution)/shard_map/reduce_scatter | solution.py:282
  638.6 166.2 %reduce-scatter.41.cloned.1.call-start = ((), (), s32[]{:S(2)}) async-start(), calls=%async_computation.38 | async-start | bytes 2621440 | tf_op jit(solution)/shard_map/reduce_scatter | solution.py:282
  642.9 189.9 %reduce-scatter.31.cloned.1.call-start = ((), (), s32[]{:S(2)}) async-start(), calls=%async_computation.33 | async-start | bytes 1310720 | tf_op jit(solution)/shard_map/reduce_scatter | solution.py:23
  665.2 196.7 %reduce-scatter.39.cloned.1.call-start = ((), (), s32[]{:S(2)}) async-start(), calls=%async_computation.37 | async-start | bytes 655360 | tf_op jit(solution)/shard_map/reduce_scatter | solution.py:282
  666.5 223.9 %reduce-scatter.37.cloned.1.call-start = ((), (), s32[]{:S(2)}) async-start(), calls=%async_computation.36 | async-start | bytes 655360 | tf_op jit(solution)/shard_map/reduce_scatter | solution.py:282
  669.2 255.2 %reduce-scatter.35.cloned.1.call-start = ((), (), s32[]{:S(2)}) async-start(), calls=%async_computation.35 | async-start | bytes 1966080 | tf_op jit(solution)/shard_map/reduce_scatter | solution.py:282
  677.6 281.0 %reduce-scatter.33.cloned.1.call-start = ((), (), s32[]{:S(2)}) async-start(), calls=%async_computation.34 | async-start | bytes 1966080 | tf_op jit(solution)/shard_map/reduce_scatter | solution.py:282
  730.6 75.4 %collective-permute-start.5 = (bf16[1024,256]{1,0:T(8,128)(2,1)}, bf16[1024,256]{1,0:T(8,128)(2,1)}, u32[]{:S(2)}, u32[]{:S(2)}) collective-permute-start(bf16[1024,256]{1,0:T(8,128)(2,1)} %broadcast_select_fusion), channel_id=1, source_target_pairs={{0,16},{16,0},{1,17},{17,1},{2,18},{18,2},{3,19},{19,3},{4,20},{20... | collective-permute-start | bytes 1572872 | tf_op jit(solution)/shard_map/ppermute | solution.py:179
  842.0 247.3 %all-reduce.3.cloned.1.call-start = ((), (), s32[]{:S(2)}) async-start(), calls=%async_computation.49 | async-start | bytes 196608
  891.4 68.4 %collective-permute-start.3 = (bf16[256,256]{1,0:T(8,128)(2,1)S(1)}, bf16[256,256]{1,0:T(8,128)(2,1)S(1)}, u32[]{:S(2)}, u32[]{:S(2)}) collective-permute-start(bf16[256,256]{1,0:T(8,128)(2,1)S(1)} %broadcast_select_fusion.3), channel_id=1, source_target_pairs={{0,16},{16,0},{1,17},{17,1},{2,18},{18,2},{3,19},{19,3},{4,20},{20... | collective-permute-start | bytes 393224 | tf_op jit(solution)/shard_map/ppermute | solution.py:179
  893.6 202.0 %collective-permute-start.1 = (bf16[512,256]{1,0:T(8,128)(2,1)S(1)}, bf16[512,256]{1,0:T(8,128)(2,1)S(1)}, u32[]{:S(2)}, u32[]{:S(2)}) collective-permute-start(bf16[512,256]{1,0:T(8,128)(2,1)S(1)} %get-tuple-element.55), channel_id=1, source_target_pairs={{0,16},{16,0},{1,17},{17,1},{2,18},{18,2},{3,19},{19,3},{4,20},{20... | collective-permute-start | bytes 786440 | tf_op jit(solution)/shard_map/ppermute | solution.py:179
  959.7 136.9 %collective-permute-start.2 = (bf16[256,4,192]{0,2,1:T(8,128)(2,1)S(1)}, bf16[256,4,192]{0,2,1:T(8,128)(2,1)S(1)}, u32[]{:S(2)}, u32[]{:S(2)}) collective-permute-start(bf16[256,4,192]{0,2,1:T(8,128)(2,1)S(1)} %broadcast_select_fusion.2), channel_id=1, source_target_pairs={{0,16},{16,0},{1,17},{17,1},{2,18},{18,2},{3,19},{19,3},{4,20},{20... | collective-permute-start | bytes 1179656 | tf_op jit(solution)/shard_map/ppermute | solution.py:179
  (67 other events, 2005.5 us)
Sparse Core Ops, SparseCore 0:
  9.8 31.8 all-gather.40
  43.9 31.0 all-gather.24
  76.6 9.6 all-gather.42
  87.6 10.1 all-gather.44
  99.6 36.1 all-gather.46
  138.5 25.9 reduce-scatter.16
  166.3 35.6 all-gather.50
  203.4 13.9 all-gather.48
  219.6 28.8 all-gather.26
  249.8 13.3 all-gather.52
  268.1 26.1 reduce-scatter.18
  296.3 28.4 all-gather.28
  339.4 24.6 reduce-scatter.20
  367.2 28.4 all-gather.30
  397.8 30.3 all-gather.32
  436.8 22.4 reduce-scatter.24
  462.0 25.7 reduce-scatter.22
  490.2 28.4 all-gather.34
  530.7 24.6 reduce-scatter.26
  558.7 28.4 all-gather.36
  595.8 24.6 reduce-scatter.28
  624.5 28.4 all-gather.38
  656.0 34.5 reduce-scatter.46
  693.4 35.1 reduce-scatter.44
  731.6 35.1 reduce-scatter.42
  769.6 35.1 reduce-scatter.40
  807.6 25.2 reduce-scatter.30
  836.2 25.6 reduce-scatter.38
  865.3 25.0 reduce-scatter.36
  893.3 31.1 reduce-scatter.34
  927.4 31.1 reduce-scatter.32
  964.8 124.4 all-reduce.2
where the time goes:
time: 1110 us; the launch traced here: 1100 us
  waiting for transfers between devices  828 us (75%)
  matrix products  101 us (9%)
  blocking collectives  75.8 us (7%)
  other arithmetic  48.3 us (4%)
  local copies, waits for them, and re-layouts  22.2 us (2%)
  between operations  15.5 us (1%)
  starting transfers between devices  13.1 us (1%)
    reduce_scatter x8, waiting for transfers between devices, reduce_big(): lax.psum_scatter(item.astype(bf16), 'seq', scatter_dimension=axis, tiled=...  220 us
    reduce_scatter x8, waiting for transfers between devices, scatter_rows(): lax.psum_scatter(partial_rows.astype(bf16), 'tensor', scatter_dimension=0...  195 us
    all_gather x6, waiting for transfers between devices, gather_rows(): return lax.all_gather(piece, 'tensor', axis=0, tiled=True)  153 us
    unnamed x33, waiting for transfers between devices  132 us
    all_gather x3, waiting for transfers between devices, pair(): gathered = lax.all_gather(weight, 'seq', axis=axis, tiled=True)  67.2 us
    dot_general x18, matrix products, dot(): lax.dot_general(left, right, (dims, ((), ())), preferred_element_type=f32)  62.8 us
    all_gather x1, blocking collectives, body(): lax.all_gather(packed, ('section', 'tensor', 'seq'), axis=0, tiled=False)  62.1 us
    all_gather x2, waiting for transfers between devices, gather_columns(): return lax.all_gather(piece, 'tensor', axis=1, tiled=True)  27.9 us
  transfers between devices with their start and end apart: 40, of which 29 were waited for; matrix products, arithmetic and copies ran while one was open for 10% of the time, Pallas kernels for 0%

commit v1 on v0

--- a/solution.py
+++ b/solution.py
@@ -11,12 +11,29 @@
 bf16 = jnp.bfloat16
 
 
+def joined_along(blocks, dim):
+    blocks = jnp.moveaxis(blocks, 0, dim)
+    shape = blocks.shape
+    return blocks.reshape(*shape[:dim], shape[dim] * shape[dim + 1], *shape[dim + 2 :])
+
+
+def gather_around(x, axis, dim):
+    devices = lax.axis_size(axis)
+    right = [(i, (i + 1) % devices) for i in range(devices)]
+    blocks = [x]
+    while len(blocks) < devices:
+        blocks.append(lax.ppermute(blocks[-1], axis, right))
+    mine = lax.axis_index(axis)
+    blocks = jnp.stack(blocks)[(mine - jnp.arange(devices)) % devices]
+    return joined_along(blocks, dim)
+
+
 def gather_columns(piece):
     return lax.all_gather(piece, "tensor", axis=1, tiled=True)
 
 
 def gather_rows(piece):
-    return lax.all_gather(piece, "tensor", axis=0, tiled=True)
+    return gather_around(piece, "tensor", 0)
 
 
 def scatter_rows(partial_rows):

time: 1110 us -> 1050 us (0.946)
  waiting for transfers between devices: 828 us -> 721 us
  starting transfers between devices: 13.1 us -> 40.3 us
  local copies, waits for them, and re-layouts: 22.2 us -> 36.4 us
    all_gather x6 -> x0, waiting for transfers between devices: 153 us -> none  [gather_rows(): return lax.all_gather(piece, 'tensor', axis=0, tiled=True)]
    ppermute x0 -> x18, waiting for transfers between devices: none -> 136 us  [gather_around(): blocks.append(lax.ppermute(blocks[-1], axis, right))]
    reduce_scatter x8, waiting for transfers between devices: 220 us -> 169 us  [reduce_big(): lax.psum_scatter(item.astype(bf16), 'seq', scatter_dimension=axis, tiled=...]
    all_gather x2, waiting for transfers between devices: 27.9 us -> 0.02 us  [gather_columns(): return lax.all_gather(piece, 'tensor', axis=1, tiled=True)]
    all_gather x4, waiting for transfers between devices: 25.7 us -> 0.07 us  [pair(): return lax.all_gather(gathered, 'section', axis=0, tiled=False)]
    ppermute x0 -> x18, starting transfers between devices: none -> 25.4 us  [gather_around(): blocks.append(lax.ppermute(blocks[-1], axis, right))]
    reduce_scatter x8, waiting for transfers between devices: 195 us -> 208 us  [scatter_rows(): lax.psum_scatter(partial_rows.astype(bf16), 'tensor', scatter_dimension=0...]
    gather x0 -> x6, local copies, waits for them, and re-layouts: none -> 11.5 us  [gather_around(): blocks = jnp.stack(blocks)[(mine - jnp.arange(devices)) % devices]]
  transfers between devices with their start and end apart: 40 -> 52, of which waited for: 29 -> 39; matrix products, arithmetic and copies ran while one was open for 10% -> 11% of each run, Pallas kernels for 0% -> 0%
where the time goes in v1:
time: 1050 us; the launch traced here: 1040 us
  waiting for transfers between devices  721 us (69%)
  matrix products  96.3 us (9%)
  blocking collectives  75.9 us (7%)
  other arithmetic  51.7 us (5%)
  starting transfers between devices  40.3 us (4%)
  local copies, waits for them, and re-layouts  36.4 us (3%)
  between operations  15.3 us (1%)
    reduce_scatter x8, waiting for transfers between devices, scatter_rows(): lax.psum_scatter(partial_rows.astype(bf16), 'tensor', scatter_dimension=0...  208 us
    reduce_scatter x8, waiting for transfers between devices, reduce_big(): lax.psum_scatter(item.astype(bf16), 'seq', scatter_dimension=axis, tiled=...  169 us
    ppermute x18, waiting for transfers between devices, gather_around(): blocks.append(lax.ppermute(blocks[-1], axis, right))  136 us
    unnamed x27, waiting for transfers between devices  129 us
    all_gather x3, waiting for transfers between devices, pair(): gathered = lax.all_gather(weight, 'seq', axis=axis, tiled=True)  68.5 us
    all_gather x1, blocking collectives, body(): lax.all_gather(packed, ('section', 'tensor', 'seq'), axis=0, tiled=False)  62.1 us
    dot_general x18, matrix products, dot(): lax.dot_general(left, right, (dims, ((), ())), preferred_element_type=f32)  61.8 us
    ppermute x18, starting transfers between devices, gather_around(): blocks.append(lax.ppermute(blocks[-1], axis, right))  25.4 us
  transfers between devices with their start and end apart: 52, of which 39 were waited for; matrix products, arithmetic and copies ran while one was open for 11% of the time, Pallas kernels for 0%

profile of v1, /device:TPU:8, one launch (start us, length us, event | category | flops | bytes accessed | tf_op | source)
XLA Modules:
  0.0 1037.2 jit_solution(4694766318803074013)
XLA Ops:
  9.1 32.7 %all-gather.23.cloned.1.call-done = bf16[1,1024,4,192]{1,3,2,0:T(8,128)(2,1)} async-done(((bf16[1,256,4,192]{1,3,2,0:T(8,128)(2,1)}), bf16[1,1024,4,192]{1,3,2,0:T(8,128)(2,1)}) %all-gather.23.cloned.1.call-update) | async-done | bytes 1572880 | tf_op jit(solution)/shard_map/all_gather | solution.py:257
  41.8 13.8 %all_gather.54 = bf16[256,1024]{1,0:T(8,128)(2,1)} all-gather(bf16[256,256]{1,0:T(8,128)(2,1)S(1)} %bitcast.290), channel_id=1, replica_groups=mesh['section'=2,'seq'=4,'tensor'=4] {'seq'}, dimensions={1}, use_global_device_ids=true | all-gather | bytes 655360 | tf_op jit(solution)/shard_map/all_gather | solution.py:257
  57.1 62.1 %all-gather.8 = bf16[32,1,768]{2,1,0:T(2,128)(2,1)S(1)} all-gather(bf16[1,1,768]{2,1,0:T(2,128)(2,1)S(1)} %reshape.958), channel_id=2, replica_groups=mesh['section'=2,'seq'=4,'tensor'=4] {'section','tensor','seq'}, dimensions={0}, use_global_device_ids=true | all-gather | bytes 50688 | tf_op jit(solution)/shard_map/all_gather | solution.py:253
  136.8 35.8 %all-gather.33.cloned.1.call-done = bf16[1,1024,1024]{2,1,0:T(8,128)(2,1)} async-done(((bf16[1,1024,256]{2,1,0:T(8,128)(2,1)}), bf16[1,1024,1024]{2,1,0:T(8,128)(2,1)}) %all-gather.33.cloned.1.call-update) | async-done | bytes 2097168 | tf_op jit(solution)/shard_map/all_gather | solution.py:257
  172.9 27.8 %reduce-scatter.17.cloned.1.call-done = bf16[128,1024]{1,0:T(8,128)(2,1)} async-done(((bf16[512,1024]{1,0:T(8,128)(2,1)}), bf16[128,1024]{1,0:T(8,128)(2,1)}) %reduce-scatter.17.cloned.1.call-update) | async-done | bytes 262160 | tf_op jit(solution)/shard_map/reduce_scatter | solution.py:40
  213.1 7.1 collective-permute-done.1
  220.9 7.2 collective-permute-done.2
  238.7 26.4 %reduce-scatter.19.cloned.1.call-done = bf16[128,1024]{1,0:T(8,128)(2,1)} async-done(((bf16[512,1024]{1,0:T(8,128)(2,1)}), bf16[128,1024]{1,0:T(8,128)(2,1)}) %reduce-scatter.19.cloned.1.call-update) | async-done | bytes 262160 | tf_op jit(solution)/shard_map/reduce_scatter | solution.py:40
  276.4 6.9 collective-permute-done.4
  284.0 7.4 collective-permute-done.5
  309.0 25.7 %reduce-scatter.21.cloned.1.call-done = bf16[128,1024]{1,0:T(8,128)(2,1)} async-done(((bf16[512,1024]{1,0:T(8,128)(2,1)}), bf16[128,1024]{1,0:T(8,128)(2,1)}) %reduce-scatter.21.cloned.1.call-update) | async-done | bytes 262160 | tf_op jit(solution)/shard_map/reduce_scatter | solution.py:40
  347.1 14.3 %collective-permute-done.7 = bf16[128,1024]{1,0:T(8,128)(2,1)S(1)} collective-permute-done((bf16[128,1024]{1,0:T(8,128)(2,1)S(1)}, bf16[128,1024]{1,0:T(8,128)(2,1)S(1)}, u32[]{:S(2)}, u32[]{:S(2)}) %collective-permute-start.7) | collective-permute-done | bytes 262176 | tf_op jit(solution)/shard_map/ppermute | solution.py:25
  363.8 11.2 %collective-permute-done.8 = bf16[128,1024]{1,0:T(8,128)(2,1)S(1)} collective-permute-done((bf16[128,1024]{1,0:T(8,128)(2,1)S(1)}, bf16[128,1024]{1,0:T(8,128)(2,1)S(1)}, u32[]{:S(2)}, u32[]{:S(2)}) %collective-permute-start.8) | collective-permute-done | bytes 262176 | tf_op jit(solution)/shard_map/ppermute | solution.py:25
  397.1 20.7 %reduce-scatter.25.cloned.1.call-done = bf16[128,1024]{1,0:T(8,128)(2,1)} async-done(((bf16[512,1024]{1,0:T(8,128)(2,1)}), bf16[128,1024]{1,0:T(8,128)(2,1)}) %reduce-scatter.25.cloned.1.call-update) | async-done | bytes 262160 | tf_op jit(solution)/shard_map/reduce_scatter | solution.py:40
  419.2 26.6 %reduce-scatter.23.cloned.1.call-done = bf16[128,1024]{1,0:T(8,128)(2,1)} async-done(((bf16[512,1024]{1,0:T(8,128)(2,1)}), bf16[128,1024]{1,0:T(8,128)(2,1)}) %reduce-scatter.23.cloned.1.call-update) | async-done | bytes 262160 | tf_op jit(solution)/shard_map/reduce_scatter | solution.py:40
  458.0 7.0 collective-permute-done.11
  465.2 7.8 collective-permute-done.12
  488.9 26.7 %reduce-scatter.27.cloned.1.call-done = bf16[128,1024]{1,0:T(8,128)(2,1)} async-done(((bf16[512,1024]{1,0:T(8,128)(2,1)}), bf16[128,1024]{1,0:T(8,128)(2,1)}) %reduce-scatter.27.cloned.1.call-update) | async-done | bytes 262160 | tf_op jit(solution)/shard_map/reduce_scatter | solution.py:40
  520.3 6.5 collective-permute-done.13
  528.3 7.1 collective-permute-done.14
  535.4 7.8 collective-permute-done.15
  553.5 26.7 %reduce-scatter.29.cloned.1.call-done = bf16[128,1024]{1,0:T(8,128)(2,1)} async-done(((bf16[512,1024]{1,0:T(8,128)(2,1)}), bf16[128,1024]{1,0:T(8,128)(2,1)}) %reduce-scatter.29.cloned.1.call-update) | async-done | bytes 262160 | tf_op jit(solution)/shard_map/reduce_scatter | solution.py:40
  594.2 7.0 collective-permute-done.17
  601.7 7.8 collective-permute-done.18
  649.5 7.2 all-to-all-start
  680.1 38.1 %reduce-scatter.45.cloned.1.call-done = bf16[1024,256]{1,0:T(8,128)(2,1)} async-done(((bf16[1024,1024]{1,0:T(8,128)(2,1)}), bf16[1024,256]{1,0:T(8,128)(2,1)}) %reduce-scatter.45.cloned.1.call-update) | async-done | bytes 524304 | tf_op jit(solution)/shard_map/reduce_scatter | solution.py:299
  720.0 36.3 %reduce-scatter.43.cloned.1.call-done = bf16[256,1024]{1,0:T(8,128)(2,1)} async-done(((bf16[1024,1024]{1,0:T(8,128)(2,1)}), bf16[256,1024]{1,0:T(8,128)(2,1)}) %reduce-scatter.43.cloned.1.call-update) | async-done | bytes 524304 | tf_op jit(solution)/shard_map/reduce_scatter | solution.py:299
  756.3 38.2 %reduce-scatter.41.cloned.1.call-done = bf16[256,1024]{1,0:T(8,128)(2,1)} async-done(((bf16[1024,1024]{1,0:T(8,128)(2,1)}), bf16[256,1024]{1,0:T(8,128)(2,1)}) %reduce-scatter.41.cloned.1.call-update) | async-done | bytes 524304 | tf_op jit(solution)/shard_map/reduce_scatter | solution.py:299
  795.7 26.9 %reduce-scatter.31.cloned.1.call-done = bf16[128,1024]{1,0:T(8,128)(2,1)} async-done(((bf16[512,1024]{1,0:T(8,128)(2,1)}), bf16[128,1024]{1,0:T(8,128)(2,1)}) %reduce-scatter.31.cloned.1.call-update) | async-done | bytes 262160 | tf_op jit(solution)/shard_map/reduce_scatter | solution.py:40
  840.5 16.7 %reduce-scatter.35.cloned.1.call-done = bf16[256,4,192]{0,2,1:T(8,128)(2,1)} async-done(((bf16[1024,4,192]{0,2,1:T(8,128)(2,1)}), bf16[256,4,192]{0,2,1:T(8,128)(2,1)}) %reduce-scatter.35.cloned.1.call-update) | async-done | bytes 393232 | tf_op jit(solution)/shard_map/reduce_scatter | solution.py:299
  857.2 34.1 %reduce-scatter.33.cloned.1.call-done = bf16[256,4,192]{0,2,1:T(8,128)(2,1)} async-done(((bf16[1024,4,192]{0,2,1:T(8,128)(2,1)}), bf16[256,4,192]{0,2,1:T(8,128)(2,1)}) %reduce-scatter.33.cloned.1.call-update) | async-done | bytes 393232 | tf_op jit(solution)/shard_map/reduce_scatter | solution.py:299
  895.5 125.8 %all-reduce.3.cloned.1.call-done = f32[32,768]{1,0:T(8,128)} async-done(((f32[32,768]{1,0:T(8,128)}), f32[32,768]{1,0:T(8,128)}) %all-reduce.3.cloned.1.call-update) | async-done | bytes 98320
  (408 shorter events, 268.6 us)
Async XLA Ops:
  7.2 34.5 %all-gather.23.cloned.1.call-start = ((), (), s32[]{:S(2)}) async-start(), calls=%async_computation.36 | async-start | bytes 1966080 | tf_op jit(solution)/shard_map/all_gather | solution.py:257
  7.9 112.5 %all-gather.19.cloned.1.call-start = ((), (), s32[]{:S(2)}) async-start(), calls=%async_computation.18 | async-start | bytes 1310720 | tf_op jit(solution)/shard_map/all_gather | solution.py:32
  9.0 113.1 %all-gather.25.cloned.1.call-start = ((), (), s32[]{:S(2)}) async-start(), calls=%async_computation.37 | async-start | bytes 4718592 | tf_op jit(solution)/shard_map/all_gather | solution.py:258
  41.8 91.7 %all-gather.27.cloned.1.call-start = ((), (), s32[]{:S(2)}) async-start(), calls=%async_computation.38 | async-start | bytes 1572864 | tf_op jit(solution)/shard_map/all_gather | solution.py:258
  55.6 80.5 %all-gather.29.cloned.1.call-start = ((), (), s32[]{:S(2)}) async-start(), calls=%async_computation.39 | async-start | bytes 2621440 | tf_op jit(solution)/shard_map/all_gather | solution.py:257
  56.2 116.4 %all-gather.33.cloned.1.call-start = ((), (), s32[]{:S(2)}) async-start(), calls=%async_computation.41 | async-start | bytes 2621440 | tf_op jit(solution)/shard_map/all_gather | solution.py:257
  56.8 144.0 %reduce-scatter.17.cloned.1.call-start = ((), (), s32[]{:S(2)}) async-start(), calls=%async_computation.19 | async-start | bytes 1310720 | tf_op jit(solution)/shard_map/reduce_scatter | solution.py:40
  136.0 92.8 %all-gather.31.cloned.1.call-start = ((), (), s32[]{:S(2)}) async-start(), calls=%async_computation.40 | async-start | bytes 6291456 | tf_op jit(solution)/shard_map/all_gather | solution.py:258
  136.8 97.0 %all-gather.35.cloned.1.call-start = ((), (), s32[]{:S(2)}) async-start(), calls=%async_computation.42 | async-start | bytes 6291456 | tf_op jit(solution)/shard_map/all_gather | solution.py:258
  172.7 92.4 %reduce-scatter.19.cloned.1.call-start = ((), (), s32[]{:S(2)}) async-start(), calls=%async_computation.20 | async-start | bytes 1310720 | tf_op jit(solution)/shard_map/reduce_scatter | solution.py:40
  238.6 96.1 %reduce-scatter.21.cloned.1.call-start = ((), (), s32[]{:S(2)}) async-start(), calls=%async_computation.21 | async-start | bytes 1310720 | tf_op jit(solution)/shard_map/reduce_scatter | solution.py:40
  307.9 75.6 %all-gather.21.cloned.1.call-start = ((), (), s32[]{:S(2)}) async-start(), calls=%async_computation.23 | async-start | bytes 1310720 | tf_op jit(solution)/shard_map/all_gather | solution.py:32
  308.7 109.2 %reduce-scatter.25.cloned.1.call-start = ((), (), s32[]{:S(2)}) async-start(), calls=%async_computation.24 | async-start | bytes 1310720 | tf_op jit(solution)/shard_map/reduce_scatter | solution.py:40
  345.5 15.8 %collective-permute-start.7 = (bf16[128,1024]{1,0:T(8,128)(2,1)S(1)}, bf16[128,1024]{1,0:T(8,128)(2,1)S(1)}, u32[]{:S(2)}, u32[]{:S(2)}) collective-permute-start(bf16[128,1024]{1,0:T(8,128)(2,1)S(1)} %collective-permute-done.6), channel_id=1, source_target_pairs={{0,1},{1,2},{2,3},{3,0},{4,5},{5,6},{6,7},{7,4},{8,9},{9,10},{10,1... | collective-permute-start | bytes 786440 | tf_op jit(solution)/shard_map/ppermute | solution.py:25
  361.3 13.7 %collective-permute-start.8 = (bf16[128,1024]{1,0:T(8,128)(2,1)S(1)}, bf16[128,1024]{1,0:T(8,128)(2,1)S(1)}, u32[]{:S(2)}, u32[]{:S(2)}) collective-permute-start(bf16[128,1024]{1,0:T(8,128)(2,1)S(1)} %collective-permute-done.7), channel_id=1, source_target_pairs={{0,1},{1,2},{2,3},{3,0},{4,5},{5,6},{6,7},{7,4},{8,9},{9,10},{10,1... | collective-permute-start | bytes 786440 | tf_op jit(solution)/shard_map/ppermute | solution.py:25
  392.0 53.9 %reduce-scatter.23.cloned.1.call-start = ((), (), s32[]{:S(2)}) async-start(), calls=%async_computation.22 | async-start | bytes 1310720 | tf_op jit(solution)/shard_map/reduce_scatter | solution.py:40
  396.8 118.9 %reduce-scatter.27.cloned.1.call-start = ((), (), s32[]{:S(2)}) async-start(), calls=%async_computation.25 | async-start | bytes 1310720 | tf_op jit(solution)/shard_map/reduce_scatter | solution.py:40
  488.9 91.4 %reduce-scatter.29.cloned.1.call-start = ((), (), s32[]{:S(2)}) async-start(), calls=%async_computation.26 | async-start | bytes 1310720 | tf_op jit(solution)/shard_map/reduce_scatter | solution.py:40
  553.5 116.8 %reduce-scatter.39.cloned.1.call-start = ((), (), s32[]{:S(2)}) async-start(), calls=%async_computation.31 | async-start | bytes 655360 | tf_op jit(solution)/shard_map/reduce_scatter | solution.py:299
  587.2 83.1 %reduce-scatter.37.cloned.1.call-start = ((), (), s32[]{:S(2)}) async-start(), calls=%async_computation.30 | async-start | bytes 655360 | tf_op jit(solution)/shard_map/reduce_scatter | solution.py:299
  614.7 65.3 %reduce-scatter.47.cloned.1.call-start = ((), (), s32[]{:S(2)}) async-start(), calls=%async_computation.35 | async-start | bytes 2621440 | tf_op jit(solution)/shard_map/reduce_scatter | solution.py:299
  619.6 98.5 %reduce-scatter.45.cloned.1.call-start = ((), (), s32[]{:S(2)}) async-start(), calls=%async_computation.34 | async-start | bytes 2621440 | tf_op jit(solution)/shard_map/reduce_scatter | solution.py:299
  624.5 131.8 %reduce-scatter.43.cloned.1.call-start = ((), (), s32[]{:S(2)}) async-start(), calls=%async_computation.33 | async-start | bytes 2621440 | tf_op jit(solution)/shard_map/reduce_scatter | solution.py:299
  628.8 165.7 %reduce-scatter.41.cloned.1.call-start = ((), (), s32[]{:S(2)}) async-start(), calls=%async_computation.32 | async-start | bytes 2621440 | tf_op jit(solution)/shard_map/reduce_scatter | solution.py:299
  633.1 189.6 %reduce-scatter.31.cloned.1.call-start = ((), (), s32[]{:S(2)}) async-start(), calls=%async_computation.27 | async-start | bytes 1310720 | tf_op jit(solution)/shard_map/reduce_scatter | solution.py:40
  645.0 212.2 %reduce-scatter.35.cloned.1.call-start = ((), (), s32[]{:S(2)}) async-start(), calls=%async_computation.29 | async-start | bytes 1966080 | tf_op jit(solution)/shard_map/reduce_scatter | solution.py:299
  656.7 234.6 %reduce-scatter.33.cloned.1.call-start = ((), (), s32[]{:S(2)}) async-start(), calls=%async_computation.28 | async-start | bytes 1966080 | tf_op jit(solution)/shard_map/reduce_scatter | solution.py:299
  720.0 111.8 %collective-permute-start.23 = (bf16[1024,256]{1,0:T(8,128)(2,1)}, bf16[1024,256]{1,0:T(8,128)(2,1)}, u32[]{:S(2)}, u32[]{:S(2)}) collective-permute-start(bf16[1024,256]{1,0:T(8,128)(2,1)} %broadcast_select_fusion), channel_id=1, source_target_pairs={{0,16},{16,0},{1,17},{17,1},{2,18},{18,2},{3,19},{19,3},{4,20},{20... | collective-permute-start | bytes 1572872 | tf_op jit(solution)/shard_map/ppermute | solution.py:196
  795.6 97.5 %collective-permute-start.22 = (bf16[256,1024]{1,0:T(8,128)(2,1)S(1)}, bf16[256,1024]{1,0:T(8,128)(2,1)}, u32[]{:S(2)}, u32[]{:S(2)}) collective-permute-start(bf16[256,1024]{1,0:T(8,128)(2,1)S(1)} %broadcast_select_fusion.1), channel_id=1, source_target_pairs={{0,16},{16,0},{1,17},{17,1},{2,18},{18,2},{3,19},{19,3},{4,20},{20... | collective-permute-start | bytes 1572872 | tf_op jit(solution)/shard_map/ppermute | solution.py:196
  831.8 189.5 %all-reduce.3.cloned.1.call-start = ((), (), s32[]{:S(2)}) async-start(), calls=%async_computation.43 | async-start | bytes 196608
  840.5 186.9 %collective-permute-start.19 = (bf16[512,256]{1,0:T(8,128)(2,1)}, bf16[512,256]{1,0:T(8,128)(2,1)}, u32[]{:S(2)}, u32[]{:S(2)}) collective-permute-start(bf16[512,256]{1,0:T(8,128)(2,1)} %get-tuple-element.55), channel_id=1, source_target_pairs={{0,16},{16,0},{1,17},{17,1},{2,18},{18,2},{3,19},{19,3},{4,20},{20... | collective-permute-start | bytes 786440 | tf_op jit(solution)/shard_map/ppermute | solution.py:196
  893.1 136.3 %collective-permute-start.20 = (bf16[256,4,192]{0,2,1:T(8,128)(2,1)}, bf16[256,4,192]{0,2,1:T(8,128)(2,1)S(1)}, u32[]{:S(2)}, u32[]{:S(2)}) collective-permute-start(bf16[256,4,192]{0,2,1:T(8,128)(2,1)} %broadcast_select_fusion.2), channel_id=1, source_target_pairs={{0,16},{16,0},{1,17},{17,1},{2,18},{18,2},{3,19},{19,3},{4,20},{20... | collective-permute-start | bytes 1179656 | tf_op jit(solution)/shard_map/ppermute | solution.py:196
  (84 other events, 1872.3 us)
Sparse Core Ops, SparseCore 0:
  9.8 31.8 all-gather.22
  43.9 31.2 all-gather.18
  76.7 9.6 all-gather.24
  87.7 10.1 all-gather.26
  99.7 36.1 all-gather.28
  137.6 35.0 all-gather.32
  175.5 25.2 reduce-scatter.16
  202.3 14.5 all-gather.30
  218.4 14.8 all-gather.34
  238.7 26.3 reduce-scatter.18
  308.0 26.6 reduce-scatter.20
  336.7 38.4 all-gather.20
  392.1 25.7 reduce-scatter.24
  420.0 25.7 reduce-scatter.22
  489.0 26.6 reduce-scatter.26
  553.6 26.6 reduce-scatter.28
  587.4 26.5 reduce-scatter.38
  616.6 25.0 reduce-scatter.36
  644.7 35.3 reduce-scatter.46
  682.9 35.2 reduce-scatter.44
  721.1 35.1 reduce-scatter.42
  759.3 35.1 reduce-scatter.40
  797.4 25.2 reduce-scatter.30
  825.5 31.6 reduce-scatter.34
  860.2 31.1 reduce-scatter.32
  896.8 124.5 all-reduce.2
